TPU v7x, 32 devices: a whole 2x2x4 slice. The times are simulated.
32 devices in a mesh: group: 2 (over x), wide: 16 (over z, y, core).
Axes of the slice: x: 2, y: 2, z: 4, core: 2. Of those that a mesh axis runs over, the one named last changes fastest.
Arguments:
- visibilities: float32 [6144, 2, 128], P(('group', 'wide')), parts along dimension 0, may hold values from -6 to 6
- offsets: float32 [6144, 2, 128], P(('group', 'wide')), parts along dimension 0, may hold values from 2 to 30
- vis_count: int32 [6144], P(('group', 'wide')), parts along dimension 0, may hold values from 1 to 128, 294912 in all
- owner: int32 [6144], P(('group', 'wide')), parts along dimension 0, may hold values from 0 to 15, as said below
- tile_row: int32 [6144], P(('group', 'wide')), parts along dimension 0, may hold values from 0 to 7
- tile_col: int32 [6144], P(('group', 'wide')), parts along dimension 0, may hold values from 0 to 127
Outputs:
- image: float32 [2, 8192, 4096], P(None, 'group', 'wide'), parts along dimension 1
There are 2 independent parts, one for each index of `group`. A program takes and returns all parts, laid end to end along the dimension named above; each array names one. Nothing has to cross between parts.
Inputs may be any that keep to these rules, and one draw needn't show every extreme that they name: At most 36 subgrids of one device have the same owner; in every draw one owner receives exactly 36 subgrids from every device. `vis_count`: the live visibilities of a subgrid are the first ones of its slots; some subgrid has all 128 live; over each part along group the counts sum to 294912.
All inputs are finite; a program needn't handle non-finite values.
Results may differ from a plain program's by a relative error of at most 0.0003.
Values sent between devices are 32-bit elements; how exact they have to be, the bound alone decides.
A program may use at most 128 MiB of HBM per device.

v0:
```python
import functools
import math

import jax
import jax.numpy as jnp
import numpy as np
from jax import lax
from jax.experimental import pallas as pl
from jax.experimental.pallas import tpu as pltpu
from jax.sharding import PartitionSpec as P

SUB = 32
HALF = SUB // 2
VIS = 128
GRID = 4096
TILES = GRID // SUB
F32 = jnp.float32
BF16 = jnp.bfloat16


def _poly_coefs():
    nodes = 0.125 * (1 + np.cos(np.pi * (np.arange(64) + 0.5) / 64))
    r = np.sqrt(nodes)
    cheb = np.polynomial.chebyshev.Chebyshev
    c = cheb.fit(nodes, np.cos(2 * np.pi * r), 5, domain=[0, 0.25])
    s = cheb.fit(nodes, np.sin(2 * np.pi * r) / r, 5, domain=[0, 0.25])
    poly = np.polynomial.Polynomial
    return (
        [float(v) for v in c.convert(kind=poly).coef],
        [float(v) for v in s.convert(kind=poly).coef],
    )


COS_C, SIN_C = _poly_coefs()


def cis(turns):
    r = turns - jnp.round(turns)
    z = r * r
    c = COS_C[5]
    s = SIN_C[5]
    for k in range(4, -1, -1):
        c = c * z + COS_C[k]
        s = s * z + SIN_C[k]
    return c, s * r


def split(x):
    hi = x.astype(BF16)
    lo = (x - hi.astype(F32)).astype(BF16)
    return hi, lo


def np_tables():
    t = np.arange(SUB)
    q = np.arange(SUB)
    n0 = np.arange(TILES)
    g = np.einsum(
        "tq,qn->tn",
        np.exp(-2j * np.pi * np.outer(t, q) / SUB),
        np.exp(-2j * np.pi * np.outer(q, n0) / GRID),
    )
    w = np.exp(-2j * np.pi * (np.outer(n0, n0) % TILES) / TILES)
    return g, w


def to_waves(g):
    up = g[:, HALF:]
    down = g[:, HALF - 1 :: -1]
    return np.concatenate([up + down, 1j * (up - down)], 1)


def shifted(g):
    index = (np.arange(SUB)[:, None] + np.arange(SUB)[None, :]) % SUB
    return to_waves(g[index])


def pixel_rows(raw_ref, size, out_ref, row_ref):
    step = (lax.broadcasted_iota(jnp.int32, (8, VIS), 0).astype(F32) + 0.5) / SUB
    lane = lax.broadcasted_iota(jnp.int32, (16, VIS), 1)
    cat = jnp.concatenate

    def prepare(t):
        ar, ai, u, v = (raw_ref[q * size + t * 8 : q * size + t * 8 + 8] for q in range(4))
        pr, pi = cis((u + v) * (-1.0 / (2 * SUB)))
        ur, ui = cis(u * 0.25)
        vr, vi = cis(v * 0.25)
        rows = [u, v, ur, ui, vr, vi, ar * pr - ai * pi, ar * pi + ai * pr]
        for q, row in enumerate(rows):
            row_ref[t, q] = row

    def wave(turns, r8, i8):
        c0, s0 = cis(turns * step)
        return [c0, c0 * r8 - s0 * i8, s0, c0 * i8 + s0 * r8]

    def one(t, d):
        bc = lambda q: jnp.broadcast_to(row_ref[t, q, d : d + 1, :], (8, VIS))
        u, v, ur, ui, vr, vi, ar, ai = (bc(q) for q in range(8))
        us = cat(wave(u, ur, ui), 0)
        vs = wave(v, vr, vi)
        bs = cat([ar * x for x in vs] + [ai * x for x in vs], 0)
        uh, ul = split(us)
        bh, bl = split(bs)
        prod = lax.dot_general(
            cat([uh, ul], 1),
            cat([cat([bh, bh], 1), cat([bl, bl], 1)], 0),
            (((1,), (1,)), ((), ())),
            preferred_element_type=F32,
        )
        q = prod + pltpu.roll(prod, 64, 1)
        out_ref[t * 8 + d] = jnp.where(lane < 64, q[:16], q[16:])

    for t in range(size // 8):
        prepare(t)
    for t in range(size // 8):
        for d in range(8):
            one(t, d)


def gather_kernel(
    wide, subs, size, lag, count_ref, vis_ref, off_ref, tile_ref, pix_hbm, ids_hbm,
    raw_ref, row_ref, out_ref,
    send_sem, recv_sem, loc_sem, pix_send, pix_recv, id_loc, id_send, id_recv,
):
    depth = wide // 4
    pieces = subs // size
    trips = 2 * depth * pieces
    me = lax.axis_index("wide")
    core, y, z = me % 2, (me // 2) % 2, me // 4
    place = lambda zz, yy, cc: (zz * 2 + yy) * 2 + cc
    partner = {"wide": place(z, y, 1 - core)}
    across = {"wide": place(z, 1 - y, core)}
    above = {"wide": place(jnp.minimum(z + 1, depth - 1), y, core)}
    below = {"wide": place(jnp.maximum(z - 1, 0), y, core)}
    not_top, not_bottom = z < depth - 1, z > 0
    mesh_id = pl.DeviceIdType.MESH
    here = z * 2 + y

    barrier = pltpu.get_barrier_semaphore()
    for peer in (partner, across):
        pl.semaphore_signal(barrier, inc=1, device_id=peer, device_id_type=mesh_id)

    @pl.when(not_top)
    def _():
        pl.semaphore_signal(barrier, inc=1, device_id=above, device_id_type=mesh_id)

    @pl.when(not_bottom)
    def _():
        pl.semaphore_signal(barrier, inc=1, device_id=below, device_id_type=mesh_id)

    slots = lax.broadcasted_iota(jnp.int32, (2, VIS), 1)

    def stage(t, carry):
        piece = t * 8 // size
        base = t * 8 - piece * size
        for d in range(8):
            n = t * 8 + d
            live = jnp.where(slots < count_ref[n], 1.0 / math.sqrt(VIS), 0.0)
            for half, pair in enumerate((vis_ref[n] * live, off_ref[n])):
                for q in range(2):
                    row = (half * 2 + q) * size + base + d
                    raw_ref[here, piece, pl.ds(row, 1), :] = pair[q : q + 1]
        return carry

    lax.fori_loop(0, subs // 8, stage, 0)
    for piece in range(pieces):
        raw_ref[here, piece, 4 * size :, :] = tile_ref[piece]
    neighbours = jnp.minimum(z, 1) + jnp.minimum(depth - 1 - z, 1)
    pl.semaphore_wait(barrier, 2 + neighbours)

    def hop(zz, yy, piece, to, way):
        chip = zz * 2 + yy
        return pltpu.make_async_remote_copy(
            src_ref=raw_ref.at[chip, piece],
            dst_ref=raw_ref.at[chip, piece],
            send_sem=send_sem.at[zz, piece, way],
            recv_sem=recv_sem.at[chip, piece],
            device_id=to,
            device_id_type=mesh_id,
        )

    def spread_out(zz, piece, act):
        act(hop(zz, y, piece, across, 2))

        @pl.when((zz <= z) & not_top)
        def _():
            act(hop(zz, y, piece, above, 0))

        @pl.when((zz >= z) & not_bottom)
        def _():
            act(hop(zz, y, piece, below, 1))

    for piece in range(pieces):
        spread_out(z, piece, lambda copy: copy.start())

    def pass_on(number):
        far, piece = number // pieces + 1, number % pieces
        for zz, inside in ((z - far, z - far >= 0), (z + far, z + far < depth)):

            @pl.when(inside)
            def _():
                hop(zz, y, piece, across, 2).wait_recv()
                spread_out(zz, piece, lambda copy: copy.start())

    def order(k):
        near = jnp.minimum(z, depth - 1 - z)
        swing = z + ((k + 1) // 2) * (1 - 2 * (k % 2))
        edge = jnp.where(z * 2 < depth - 1, k, depth - 1 - k)
        return jnp.where(k <= 2 * near, swing, edge)

    def copies(number, chip, piece):
        rows = pl.ds((chip * 2 + core) * subs + piece * size, size)
        slot = number % 2
        mine = pltpu.make_async_copy(out_ref.at[slot], pix_hbm.at[rows], loc_sem.at[slot])
        theirs = pltpu.make_async_remote_copy(
            src_ref=out_ref.at[slot],
            dst_ref=pix_hbm.at[rows],
            send_sem=pix_send.at[slot],
            recv_sem=pix_recv.at[number],
            device_id=partner,
            device_id_type=mesh_id,
        )
        return mine, theirs

    def id_copies(number, chip, piece):
        block = raw_ref.at[chip, piece, pl.ds(4 * size, 8)]
        where = ids_hbm.at[(chip * 2 + core) * pieces + piece]
        mine = pltpu.make_async_copy(block, where, id_loc.at[number])
        theirs = pltpu.make_async_remote_copy(
            src_ref=block,
            dst_ref=where,
            send_sem=id_send.at[number],
            recv_sem=id_recv.at[number],
            device_id=partner,
            device_id_type=mesh_id,
        )
        return mine, theirs

    def body(number, carry):
        s, piece = number // pieces, number % pieces
        zz = order(s // 2)
        yy = y + (s % 2) * (1 - 2 * y)
        chip = zz * 2 + yy

        @pl.when(s % 2 == 1)
        def _():
            hop(zz, yy, piece, across, 2).wait_recv()

        for copy in id_copies(number, chip, piece):
            copy.start()

        @pl.when(number >= 2)
        def _():
            mine, theirs = copies(number, chip, piece)
            mine.wait()
            theirs.wait_send()

        pixel_rows(raw_ref.at[chip, piece], size, out_ref.at[number % 2], row_ref)
        for copy in copies(number, chip, piece):
            copy.start()

        @pl.when((number >= lag) & (number < lag + (depth - 1) * pieces))
        def _():
            pass_on(number - lag)

        return carry

    lax.fori_loop(0, trips, body, 0)

    def drain(number, carry):
        spread_out(number // pieces, number % pieces, lambda copy: copy.wait_send())
        return carry

    lax.fori_loop(0, depth * pieces, drain, 0)
    for number in range(2):
        mine, theirs = copies(number, here, 0)
        mine.wait()
        theirs.wait_send()

    def arrive(number, carry):
        mine, theirs = id_copies(number, here, 0)
        mine.wait()
        theirs.wait()
        copies(number, here, 0)[1].wait_recv()
        return carry

    lax.fori_loop(0, trips, arrive, 0)


def gather(counts, visibilities, offsets, tile, wide, size):
    subs = visibilities.shape[0]
    depth = wide // 4
    pieces = subs // size
    trips = 2 * depth * pieces
    dma = pltpu.SemaphoreType.DMA
    anywhere = pl.BlockSpec(memory_space=pl.ANY)
    whole = pl.BlockSpec(memory_space=pltpu.VMEM)
    return pl.pallas_call(
        functools.partial(gather_kernel, wide, subs, size, min(4, 2 * pieces - 1)),
        out_shape=[
            jax.ShapeDtypeStruct((wide * subs, 16, 128), F32),
            jax.ShapeDtypeStruct((wide * pieces, 8, 128), F32),
        ],
        in_specs=[pl.BlockSpec(memory_space=pltpu.SMEM), whole, whole, whole],
        out_specs=[anywhere, anywhere],
        scratch_shapes=[
            pltpu.VMEM((wide // 2, pieces, 4 * size + 8, 128), F32),
            pltpu.VMEM((size // 8, 8, 8, VIS), F32),
            pltpu.VMEM((2, size, 16, 128), F32),
            dma((depth, pieces, 3)),
            dma((wide // 2, pieces)),
            dma((2,)),
            dma((2,)),
            dma((trips,)),
            dma((trips,)),
            dma((trips,)),
            dma((trips,)),
        ],
        compiler_params=pltpu.CompilerParams(collective_id=0, has_side_effects=True),
        name="gather",
    )(counts, visibilities, offsets, tile)


def fft(xs):
    n = len(xs)
    if n == 1:
        return xs
    even, odd = fft(xs[::2]), fft(xs[1::2])
    low, high = [], []
    root = math.sqrt(0.5)
    for k, ((er, ei), (r, i)) in enumerate(zip(even, odd)):
        if k == 0:
            tr, ti = r, i
        elif 4 * k == n:
            low.append((er + i, ei - r))
            high.append((er - i, ei + r))
            continue
        elif 8 * k == n:
            tr, ti = (r + i) * root, (i - r) * root
        elif 8 * k == 3 * n:
            tr, ti = (i - r) * root, (r + i) * -root
        else:
            tr, ti = turn(r, i, k / n)
        low.append((er + tr, ei + ti))
        high.append((er - tr, ei - ti))
    return low + high


def turn(r, i, turns):
    c, s = math.cos(2 * math.pi * turns), math.sin(2 * math.pi * turns)
    return r * c + i * s, i * c - r * s


def finish_kernel(
    block, nc, shift, p_ref, ids_ref, phr_ref, phi_ref, waves_hbm, mix_hbm, out_hbm,
    x_ref, b_ref, y_ref, tab_ref, wave_ref, mix_ref, idv_ref, ids_smem, sem, id_sem, mix_sem,
):
    g = pl.program_id(0)
    steps = pl.num_programs(0)
    halves = nc // 128
    chunk = 16
    rows = chunk * 16

    @pl.when(g == 0)
    def _():
        first = lax.axis_index("wide") * halves
        pltpu.make_async_copy(mix_hbm, mix_ref, mix_sem).start()
        load = pltpu.make_async_copy(waves_hbm.at[pl.ds(first, halves)], wave_ref, sem)
        load.start()

        def number(t, carry):
            idv_ref[pl.ds(t, 1), :] = ids_ref[t, 0:1, :].astype(jnp.int32)
            return carry

        lax.fori_loop(0, ids_ref.shape[0], number, 0, unroll=4)
        scalars = pltpu.make_async_copy(idv_ref, ids_smem, id_sem)
        scalars.start()

        def zero(t, carry):
            for lt in range(2 * halves):
                for ref in (b_ref, x_ref):
                    ref[lt, pl.ds(t * 32, 32), :] = jnp.zeros((32, 128), F32)
            return carry

        lax.fori_loop(0, TILES, zero, 0)
        load.wait()
        tab_ref[192:256] = jnp.zeros((64, 2 * nc), BF16)
        for n in range(halves):
            left = slice(n * 128, n * 128 + 128)
            right = slice(nc + n * 128, nc + n * 128 + 128)
            for part in range(3):
                dr = wave_ref[n, part // 2 * 64 : part // 2 * 64 + 32]
                di = wave_ref[n, part // 2 * 64 + 32 : part // 2 * 64 + 64]
                tab_ref[part * 64 : part * 64 + 32, left] = dr
                tab_ref[part * 64 + 32 : part * 64 + 64, left] = -di
                tab_ref[part * 64 : part * 64 + 32, right] = di
                tab_ref[part * 64 + 32 : part * 64 + 64, right] = dr
        scalars.wait()

    lane = lax.broadcasted_iota(jnp.int32, (rows, 128), 1)

    def multiply(t, slot):
        p = p_ref[pl.ds(t * chunk, chunk)].reshape(rows, 128)
        hi = p.astype(BF16)
        hif = hi.astype(F32)
        lof = p - hif
        hir = pltpu.roll(hif, 64, 1)
        lor = pltpu.roll(lof, 64, 1)
        one = jnp.where(lane < 64, hif, lor).astype(BF16)
        two = jnp.where(lane < 64, hir, lof).astype(BF16)
        lhs = jnp.concatenate(
            [
                jnp.concatenate([one, hi], 1),
                jnp.concatenate([two, hir.astype(BF16)], 1),
            ],
            0,
        )
        y_ref[slot] = jnp.dot(lhs, tab_ref[...], preferred_element_type=F32)

    def add(t, slot):
        for d in range(chunk):
            tile = ids_smem[g, t * chunk + d]
            r = lax.shift_right_logical(tile, shift)
            c = lax.bitwise_and(tile, TILES - 1)
            pr = jnp.broadcast_to(phr_ref[pl.ds(c, 1), :], (8, 128))
            pi = jnp.broadcast_to(phi_ref[pl.ds(c, 1), :], (8, 128))
            dst = pl.ds(pl.multiple_of(r * 32, 32), 32)
            acc = b_ref if d % 2 else x_ref
            old = acc[:, dst, :]
            tops = y_ref[slot, pl.ds(d * 16, 16), :]
            bots = y_ref[slot, pl.ds(rows + d * 16, 16), :]
            y = jnp.concatenate([tops, bots], 0)
            real, imag = [], []
            for n in range(halves):
                yr = y[:, n * 128 : n * 128 + 128].reshape(4, 8, 128)
                yi = y[:, nc + n * 128 : nc + n * 128 + 128].reshape(4, 8, 128)
                real.append((yr * pr - yi * pi).reshape(1, 32, 128))
                imag.append((yr * pi + yi * pr).reshape(1, 32, 128))
            acc[:, dst, :] = old + jnp.concatenate(real + imag, 0)

    trips = block // chunk
    multiply(0, 0)
    for t in range(trips):
        if t + 1 < trips:
            multiply(t + 1, (t + 1) % 2)
        add(t, t % 2)

    @pl.when(g == steps - 1)
    def _():
        at = lambda r, it: pl.ds(pl.multiple_of(r * 32 + it * 8, 8), 8)

        def eights(t, carry):
            n, it = t // 4, t % 4
            for b in range(16):
                xs = []
                for a in range(8):
                    pick = at(16 * a + b, it)
                    xs.append(
                        tuple(
                            x_ref[o * halves + n, pick, :] + b_ref[o * halves + n, pick, :]
                            for o in range(2)
                        )
                    )
                for k, (r, i) in enumerate(fft(xs)):
                    if b * k:
                        r, i = turn(r, i, b * k / TILES)
                    pick = at(16 * k + b, it)
                    x_ref[n, pick, :] = r
                    x_ref[halves + n, pick, :] = i
            return carry

        def sixteens(t, carry):
            n, it = t // 4, t % 4
            for a in range(8):
                xs = []
                for b in range(16):
                    pick = at(16 * a + b, it)
                    xs.append((x_ref[n, pick, :], x_ref[halves + n, pick, :]))
                for k, (r, i) in enumerate(fft(xs)):
                    pick = at(a + 8 * k, it)
                    b_ref[n, pick, :] = r
                    b_ref[halves + n, pick, :] = i
            return carry

        lax.fori_loop(0, 4 * halves, eights, 0)
        lax.fori_loop(0, 4 * halves, sixteens, 0)
        pltpu.make_async_copy(mix_hbm, mix_ref, mix_sem).wait()

        def mix(m, carry):
            near = pl.ds(pl.multiple_of(m * SUB, SUB), SUB)
            far = pl.ds(m, SUB, stride=TILES)
            zm = jnp.concatenate(
                [
                    jnp.concatenate([b_ref[o * halves + n, near, :] for n in range(halves)], 1)
                    for o in range(2)
                ],
                0,
            )
            zh, zl = split(zm)
            both = mix_ref[m]
            res = jnp.dot(
                jnp.concatenate([both, both[:, :64]], 1),
                jnp.concatenate([zh, zh, zl], 0),
                preferred_element_type=F32,
            )
            for p in range(2):
                for n in range(halves):
                    x_ref[p * halves + n, far, :] = res[
                        p * 32 : p * 32 + 32, n * 128 : n * 128 + 128
                    ]
            return carry

        lax.fori_loop(0, TILES, mix, 0, unroll=8)
        stores = [
            pltpu.make_async_copy(
                x_ref.at[p * halves + n],
                out_hbm.at[p, :, pl.ds(n * 128, 128)],
                sem,
            )
            for p in range(2)
            for n in range(halves)
        ]
        for store in stores:
            store.start()
        for store in stores:
            store.wait()


def finish(pix, ids, phr, phi, waves, mix, nc, block):
    count = pix.shape[0]
    tiles = 2 * nc // 128
    const = lambda shape: pl.BlockSpec(shape, lambda g: (0,) * len(shape))
    anywhere = pl.BlockSpec(memory_space=pl.ANY)
    x_shape = (tiles, GRID, 128)
    dma = pltpu.SemaphoreType.DMA
    return pl.pallas_call(
        functools.partial(finish_kernel, block, nc, TILES.bit_length() - 1),
        out_shape=jax.ShapeDtypeStruct((2, GRID, nc), F32),
        grid=(count // block,),
        in_specs=[
            pl.BlockSpec((block, 16, 128), lambda g: (g, 0, 0)),
            const(ids.shape),
            const(phr.shape),
            const(phi.shape),
            anywhere,
            anywhere,
        ],
        out_specs=anywhere,
        scratch_shapes=[
            pltpu.VMEM(x_shape, F32),
            pltpu.VMEM(x_shape, F32),
            pltpu.VMEM((2, 512, 2 * nc), F32),
            pltpu.VMEM((256, 2 * nc), BF16),
            pltpu.VMEM((nc // 128, 128, 128), BF16),
            pltpu.VMEM(mix.shape, BF16),
            pltpu.VMEM((count // block, 128), jnp.int32),
            pltpu.SMEM((count // block, 128), jnp.int32),
            dma,
            dma,
            dma,
        ],
        name="finish",
    )(pix, ids, phr, phi, waves, mix)


def np_split(x):
    hi = x.astype(np.float32).astype(BF16)
    return hi, (x - hi.astype(np.float64)).astype(BF16)


def column_waves(g):
    waves = shifted(g) / 512.0
    rh, rl = np_split(waves.real)
    ih, il = np_split(waves.imag)
    return np.concatenate([rh, ih, rl, il], 1)


def real_form(z):
    return np.array([[z.real, -z.imag], [z.imag, z.real]])


def per_device(visibilities, offsets, vis_count, owner, tile_row, tile_col):
    wide = lax.axis_size("wide")
    nc = GRID // wide
    band = GRID // (SUB * wide)
    g, w = np_tables()
    subs = visibilities.shape[0]
    size = math.gcd(subs, 64)
    tile = ((owner * band + tile_row) * TILES + tile_col).astype(F32)
    tile = jnp.pad(tile.reshape(subs // size, 1, size), ((0, 0), (0, 7), (0, 128 - size)))
    pix, ids = gather(vis_count, visibilities, offsets, tile, wide, size)
    m4 = real_form(shifted(g) / 256.0).transpose(4, 0, 2, 1, 3).reshape(TILES, 64, 64)
    both = jnp.asarray(np.concatenate(np_split(m4), 2))
    phr, phi = jnp.asarray(w.real, F32), jnp.asarray(w.imag, F32)
    return finish(pix, ids, phr, phi, jnp.asarray(column_waves(g)), both, nc, size)


def solution(mesh):
    placed = (
        P(("group", "wide"), None, None),
        P(("group", "wide"), None, None),
        P(("group", "wide")),
        P(("group", "wide")),
        P(("group", "wide")),
        P(("group", "wide")),
    )
    return jax.shard_map(
        per_device, mesh=mesh, in_specs=placed, out_specs=P(None, "group", "wide"), check_vma=False
    )
```

profile of v0, /device:TPU:0, one launch (start us, length us, event | category | flops | bytes accessed | tf_op | source)
XLA Modules:
  0.0 127.9 jit_solution(14803766450620198076)
XLA Ops:
  0.0 0.7 add_convert_fusion
  0.7 0.1 reshape.3
  0.8 0.6 pad.4.tile_ref
  1.4 55.7 %gather.1 = (f32[3072,16,128]{2,1,0:T(8,128)}, f32[48,8,128]{2,1,0:T(8,128)}) custom-call(s32[192]{0:T(256)} %count_ref.1, f32[192,2,128]{2,1,0:T(2,128)} %vis_ref.1, f32[192,2,128]{2,1,0:T(2,128)} %off_ref.1, f32[3,8,128]{2,1,0:T(8,128)} %pad.4.tile_ref), custom_call_target="tpu_custom_call" | custom-call | tf_op jit(solution)/shard_map/gather/pallas_call | solution.py:298
  57.1 70.8 %finish.1 = f32[2,4096,256]{2,1,0:T(8,128)} custom-call(f32[3072,16,128]{2,1,0:T(8,128)} %get-tuple-element.7.p_ref, f32[48,8,128]{2,1,0:T(8,128)} %get-tuple-element.8.ids_ref, f32[128,128]{1,0:T(8,128)} %constant.16.clone.phr_ref, f32[128,128]{1,0:T(8,128)} %constant.17.clone.phi_ref, bf16[32,128,128]{2,1,0:T(8,128)(2,1)} %constant.18.clone.waves_hbm, ...), custom_call_target="tpu_custom_call" | custom-call | tf_op jit(solution)/shard_map/finish/pallas_call | solution.py:536
where the time goes:
time: 130 us; the launch traced here: 128 us
  Pallas kernels  126 us (97%)
    pallas_call x1, Pallas kernels, finish(): pl.pallas_call(functools.partial(finish_kernel, block, nc, TILES.bit_leng...  70.8 us
    pallas_call x1, Pallas kernels, gather(): pl.pallas_call(functools.partial(gather_kernel, wide, subs, size, min(4,...  55.7 us

commit v1 on v0

--- a/solution.py
+++ b/solution.py
@@ -19,11 +19,12 @@
 
 
 def _poly_coefs():
-    nodes = 0.125 * (1 + np.cos(np.pi * (np.arange(64) + 0.5) / 64))
+    top = ((SUB - 4) / 2 / (2 * SUB)) ** 2
+    nodes = top / 2 * (1 + np.cos(np.pi * (np.arange(64) + 0.5) / 64))
     r = np.sqrt(nodes)
     cheb = np.polynomial.chebyshev.Chebyshev
-    c = cheb.fit(nodes, np.cos(2 * np.pi * r), 5, domain=[0, 0.25])
-    s = cheb.fit(nodes, np.sin(2 * np.pi * r) / r, 5, domain=[0, 0.25])
+    c = cheb.fit(nodes, np.cos(2 * np.pi * r), 4, domain=[0, top])
+    s = cheb.fit(nodes, np.sin(2 * np.pi * r) / r, 4, domain=[0, top])
     poly = np.polynomial.Polynomial
     return (
         [float(v) for v in c.convert(kind=poly).coef],
@@ -34,15 +35,18 @@
 COS_C, SIN_C = _poly_coefs()
 
 
-def cis(turns):
-    r = turns - jnp.round(turns)
+def cis(r):
     z = r * r
-    c = COS_C[5]
-    s = SIN_C[5]
-    for k in range(4, -1, -1):
+    c = COS_C[4]
+    s = SIN_C[4]
+    for k in range(3, -1, -1):
         c = c * z + COS_C[k]
         s = s * z + SIN_C[k]
     return c, s * r
+
+
+def cmul(a, b):
+    return a[0] * b[0] - a[1] * b[1], a[0] * b[1] + a[1] * b[0]
 
 
 def split(x):
@@ -65,8 +69,9 @@
 
 
 def to_waves(g):
-    up = g[:, HALF:]
-    down = g[:, HALF - 1 :: -1]
+    sign = (-1.0) ** np.arange(HALF)[None, :, None]
+    up = g[:, HALF:] * sign
+    down = g[:, HALF - 1 :: -1] * -sign
     return np.concatenate([up + down, 1j * (up - down)], 1)
 
 
@@ -75,51 +80,64 @@
     return to_waves(g[index])
 
 
-def pixel_rows(raw_ref, size, out_ref, row_ref):
-    step = (lax.broadcasted_iota(jnp.int32, (8, VIS), 0).astype(F32) + 0.5) / SUB
-    lane = lax.broadcasted_iota(jnp.int32, (16, VIS), 1)
+def pixel_rows(raw_ref, size, out_ref, row_ref, wave_ref):
+    lane = lax.broadcasted_iota(jnp.int32, (SUB, VIS), 1)
     cat = jnp.concatenate
 
     def prepare(t):
         ar, ai, u, v = (raw_ref[q * size + t * 8 : q * size + t * 8 + 8] for q in range(4))
-        pr, pi = cis((u + v) * (-1.0 / (2 * SUB)))
-        ur, ui = cis(u * 0.25)
-        vr, vi = cis(v * 0.25)
-        rows = [u, v, ur, ui, vr, vi, ar * pr - ai * pi, ar * pi + ai * pr]
+        firsts, steps = [], []
+        for axis, offset in enumerate((u, v)):
+            base = cis((offset - HALF) * (1.0 / (2 * SUB)))
+            twice = cmul(base, base)
+            wave = base
+            for m in range(8):
+                if m:
+                    wave = cmul(wave, twice)
+                for part in range(2):
+                    row = t * 8 * SUB + (axis * 2 + part) * 8 + m
+                    wave_ref[pl.ds(row, 8, stride=SUB), :] = wave[part]
+            firsts.append(base)
+            steps.append(cmul(wave, base))
+        pr, pi = cmul(*firsts)
+        rows = [*steps[0], *steps[1], ar * pr + ai * pi, ai * pr - ar * pi]
         for q, row in enumerate(rows):
             row_ref[t, q] = row
 
-    def wave(turns, r8, i8):
-        c0, s0 = cis(turns * step)
-        return [c0, c0 * r8 - s0 * i8, s0, c0 * i8 + s0 * r8]
-
-    def one(t, d):
+    def parts(n):
+        t, d = n // 8, n % 8
         bc = lambda q: jnp.broadcast_to(row_ref[t, q, d : d + 1, :], (8, VIS))
-        u, v, ur, ui, vr, vi, ar, ai = (bc(q) for q in range(8))
-        us = cat(wave(u, ur, ui), 0)
-        vs = wave(v, vr, vi)
-        bs = cat([ar * x for x in vs] + [ai * x for x in vs], 0)
-        uh, ul = split(us)
-        bh, bl = split(bs)
+        ur, ui, vr, vi, ar, ai = (bc(q) for q in range(6))
+        cu, su, cv, sv = (wave_ref[n * SUB + q * 8 : n * SUB + q * 8 + 8] for q in range(4))
+        ahead = lambda c, s, r, i: [c, c * r - s * i, s, c * i + s * r]
+        us = ahead(cu, su, ur, ui)
+        vs = ahead(cv, sv, vr, vi)
+        bs = [ar * x for x in vs] + [ai * x for x in vs]
+        uh, ul = split(cat(us, 0))
+        bh, bl = split(cat(bs, 0))
+        return cat([uh, ul, uh], 1), cat([bh, bh, bl], 1)
+
+    def pair(n):
+        one, two = parts(n), parts(n + 1)
         prod = lax.dot_general(
-            cat([uh, ul], 1),
-            cat([cat([bh, bh], 1), cat([bl, bl], 1)], 0),
+            cat([one[0], two[0]], 0),
+            cat([one[1], two[1]], 0),
             (((1,), (1,)), ((), ())),
             preferred_element_type=F32,
         )
-        q = prod + pltpu.roll(prod, 64, 1)
-        out_ref[t * 8 + d] = jnp.where(lane < 64, q[:16], q[16:])
-
+        out_ref[n // 2] = jnp.where(lane < 64, prod[:SUB], prod[SUB:])
+
+    prepare(0)
     for t in range(size // 8):
-        prepare(t)
-    for t in range(size // 8):
-        for d in range(8):
-            one(t, d)
+        if t + 1 < size // 8:
+            prepare(t + 1)
+        for d in range(0, 8, 2):
+            pair(t * 8 + d)
 
 
 def gather_kernel(
     wide, subs, size, lag, count_ref, vis_ref, off_ref, tile_ref, pix_hbm, ids_hbm,
-    raw_ref, row_ref, out_ref,
+    raw_ref, row_ref, wave_ref, out_ref,
     send_sem, recv_sem, loc_sem, pix_send, pix_recv, id_loc, id_send, id_recv,
 ):
     depth = wide // 4
@@ -209,7 +227,7 @@
         return jnp.where(k <= 2 * near, swing, edge)
 
     def copies(number, chip, piece):
-        rows = pl.ds((chip * 2 + core) * subs + piece * size, size)
+        rows = pl.ds(((chip * 2 + core) * subs + piece * size) // 2, size // 2)
         slot = number % 2
         mine = pltpu.make_async_copy(out_ref.at[slot], pix_hbm.at[rows], loc_sem.at[slot])
         theirs = pltpu.make_async_remote_copy(
@@ -255,7 +273,7 @@
             mine.wait()
             theirs.wait_send()
 
-        pixel_rows(raw_ref.at[chip, piece], size, out_ref.at[number % 2], row_ref)
+        pixel_rows(raw_ref.at[chip, piece], size, out_ref.at[number % 2], row_ref, wave_ref)
         for copy in copies(number, chip, piece):
             copy.start()
 
@@ -298,15 +316,16 @@
     return pl.pallas_call(
         functools.partial(gather_kernel, wide, subs, size, min(4, 2 * pieces - 1)),
         out_shape=[
-            jax.ShapeDtypeStruct((wide * subs, 16, 128), F32),
+            jax.ShapeDtypeStruct((wide * subs // 2, SUB, 128), F32),
             jax.ShapeDtypeStruct((wide * pieces, 8, 128), F32),
         ],
         in_specs=[pl.BlockSpec(memory_space=pltpu.SMEM), whole, whole, whole],
         out_specs=[anywhere, anywhere],
         scratch_shapes=[
             pltpu.VMEM((wide // 2, pieces, 4 * size + 8, 128), F32),
-            pltpu.VMEM((size // 8, 8, 8, VIS), F32),
-            pltpu.VMEM((2, size, 16, 128), F32),
+            pltpu.VMEM((size // 8, 6, 8, VIS), F32),
+            pltpu.VMEM((size * SUB, VIS), F32),
+            pltpu.VMEM((2, size // 2, SUB, 128), F32),
             dma((depth, pieces, 3)),
             dma((wide // 2, pieces)),
             dma((2,)),
@@ -353,7 +372,7 @@
 
 def finish_kernel(
     block, nc, shift, p_ref, ids_ref, phr_ref, phi_ref, waves_hbm, mix_hbm, out_hbm,
-    x_ref, b_ref, y_ref, tab_ref, wave_ref, mix_ref, idv_ref, ids_smem, sem, id_sem, mix_sem,
+    x_ref, b_ref, y_ref, tab_ref, wave_ref, mix_ref, idv_ref, ids_smem, sem, id_sem, mix_sem, out_sem,
 ):
     g = pl.program_id(0)
     steps = pl.num_programs(0)
@@ -400,18 +419,19 @@
     lane = lax.broadcasted_iota(jnp.int32, (rows, 128), 1)
 
     def multiply(t, slot):
-        p = p_ref[pl.ds(t * chunk, chunk)].reshape(rows, 128)
+        p = p_ref[pl.ds(t * chunk // 2, chunk // 2)].reshape(rows, 128)
         hi = p.astype(BF16)
         hif = hi.astype(F32)
         lof = p - hif
-        hir = pltpu.roll(hif, 64, 1)
-        lor = pltpu.roll(lof, 64, 1)
-        one = jnp.where(lane < 64, hif, lor).astype(BF16)
-        two = jnp.where(lane < 64, hir, lof).astype(BF16)
+        lo = lof.astype(BF16)
+        hir = pltpu.roll(hi, 64, 1)
+        lor = pltpu.roll(lo, 64, 1)
+        one = jnp.where(lane < 64, hi, lor)
+        two = jnp.where(lane < 64, hir, lo)
         lhs = jnp.concatenate(
             [
                 jnp.concatenate([one, hi], 1),
-                jnp.concatenate([two, hir.astype(BF16)], 1),
+                jnp.concatenate([two, hir], 1),
             ],
             0,
         )
@@ -427,9 +447,7 @@
             dst = pl.ds(pl.multiple_of(r * 32, 32), 32)
             acc = b_ref if d % 2 else x_ref
             old = acc[:, dst, :]
-            tops = y_ref[slot, pl.ds(d * 16, 16), :]
-            bots = y_ref[slot, pl.ds(rows + d * 16, 16), :]
-            y = jnp.concatenate([tops, bots], 0)
+            y = y_ref[slot, pl.ds(d % 2 * rows + d // 2 * SUB, SUB), :]
             real, imag = [], []
             for n in range(halves):
                 yr = y[:, n * 128 : n * 128 + 128].reshape(4, 8, 128)
@@ -482,52 +500,51 @@
                     b_ref[halves + n, pick, :] = i
             return carry
 
-        lax.fori_loop(0, 4 * halves, eights, 0)
-        lax.fori_loop(0, 4 * halves, sixteens, 0)
-        pltpu.make_async_copy(mix_hbm, mix_ref, mix_sem).wait()
-
-        def mix(m, carry):
-            near = pl.ds(pl.multiple_of(m * SUB, SUB), SUB)
-            far = pl.ds(m, SUB, stride=TILES)
-            zm = jnp.concatenate(
-                [
-                    jnp.concatenate([b_ref[o * halves + n, near, :] for n in range(halves)], 1)
-                    for o in range(2)
-                ],
-                0,
-            )
-            zh, zl = split(zm)
-            both = mix_ref[m]
-            res = jnp.dot(
-                jnp.concatenate([both, both[:, :64]], 1),
-                jnp.concatenate([zh, zh, zl], 0),
-                preferred_element_type=F32,
-            )
+        def mix(n, t, carry):
+            parts = []
+            for d in range(8):
+                m = t * 8 + d
+                near = pl.ds(pl.multiple_of(m * SUB, SUB), SUB)
+                zh, zl = split(
+                    jnp.concatenate([b_ref[o * halves + n, near, :] for o in range(2)], 0)
+                )
+                both = mix_ref[m]
+                res = jnp.dot(
+                    jnp.concatenate([both, both[:, :64]], 1),
+                    jnp.concatenate([zh, zh, zl], 0),
+                    preferred_element_type=F32,
+                )
+                parts.append(res[None])
+            for q in range(8):
+                block8 = jnp.concatenate([p[:, q * 8 : q * 8 + 8] for p in parts], 0)
+                turned = jnp.transpose(block8, (1, 0, 2))
+                for e in range(8):
+                    p, b = divmod(q * 8 + e, SUB)
+                    far = pl.ds(pl.multiple_of(b * TILES + t * 8, 8), 8)
+                    x_ref[p * halves + n, far, :] = turned[e]
+            return carry
+
+        stores = []
+        for n in range(halves):
+            lax.fori_loop(4 * n, 4 * n + 4, eights, 0)
+            lax.fori_loop(4 * n, 4 * n + 4, sixteens, 0)
+            if n == 0:
+                pltpu.make_async_copy(mix_hbm, mix_ref, mix_sem).wait()
+            lax.fori_loop(0, TILES // 8, functools.partial(mix, n), 0)
             for p in range(2):
-                for n in range(halves):
-                    x_ref[p * halves + n, far, :] = res[
-                        p * 32 : p * 32 + 32, n * 128 : n * 128 + 128
-                    ]
-            return carry
-
-        lax.fori_loop(0, TILES, mix, 0, unroll=8)
-        stores = [
-            pltpu.make_async_copy(
-                x_ref.at[p * halves + n],
-                out_hbm.at[p, :, pl.ds(n * 128, 128)],
-                sem,
-            )
-            for p in range(2)
-            for n in range(halves)
-        ]
-        for store in stores:
-            store.start()
+                store = pltpu.make_async_copy(
+                    x_ref.at[p * halves + n],
+                    out_hbm.at[p, :, pl.ds(n * 128, 128)],
+                    out_sem.at[p * halves + n],
+                )
+                store.start()
+                stores.append(store)
         for store in stores:
             store.wait()
 
 
 def finish(pix, ids, phr, phi, waves, mix, nc, block):
-    count = pix.shape[0]
+    count = pix.shape[0] * 2
     tiles = 2 * nc // 128
     const = lambda shape: pl.BlockSpec(shape, lambda g: (0,) * len(shape))
     anywhere = pl.BlockSpec(memory_space=pl.ANY)
@@ -538,7 +555,7 @@
         out_shape=jax.ShapeDtypeStruct((2, GRID, nc), F32),
         grid=(count // block,),
         in_specs=[
-            pl.BlockSpec((block, 16, 128), lambda g: (g, 0, 0)),
+            pl.BlockSpec((block // 2, SUB, 128), lambda g: (g, 0, 0)),
             const(ids.shape),
             const(phr.shape),
             const(phi.shape),
@@ -558,6 +575,7 @@
             dma,
             dma,
             dma,
+            dma((tiles,)),
         ],
         name="finish",
     )(pix, ids, phr, phi, waves, mix)
@@ -585,7 +603,7 @@
     band = GRID // (SUB * wide)
     g, w = np_tables()
     subs = visibilities.shape[0]
-    size = math.gcd(subs, 64)
+    size = math.gcd(subs, 96)
     tile = ((owner * band + tile_row) * TILES + tile_col).astype(F32)
     tile = jnp.pad(tile.reshape(subs // size, 1, size), ((0, 0), (0, 7), (0, 128 - size)))
     pix, ids = gather(vis_count, visibilities, offsets, tile, wide, size)

time: 130 us -> 117 us (0.900); the launches traced: 128 us -> 117 us
  Pallas kernels: 126 us -> 115 us
    pallas_call x1, Pallas kernels: 70.8 us -> 59.6 us  [finish(): pl.pallas_call(functools.partial(finish_kernel, block, nc, TILES.bit_leng...]
where the time goes in v1:
time: 117 us
  Pallas kernels  115 us (98%)
    pallas_call x1, Pallas kernels, finish(): pl.pallas_call(functools.partial(finish_kernel, block, nc, TILES.bit_leng...  59.6 us
    pallas_call x1, Pallas kernels, gather(): pl.pallas_call(functools.partial(gather_kernel, wide, subs, size, min(4,...  55.8 us

profile of v1, /device:TPU:0, one launch (start us, length us, event | category | flops | bytes accessed | tf_op | source)
XLA Modules:
  0.0 116.8 jit_solution(15139980113361527527)
XLA Ops:
  0.0 0.7 add_convert_fusion
  0.7 0.1 reshape.3
  0.8 0.6 pad.4.tile_ref
  1.4 55.8 %gather.1 = (f32[1536,32,128]{2,1,0:T(8,128)}, f32[32,8,128]{2,1,0:T(8,128)}) custom-call(s32[192]{0:T(256)} %count_ref.1, f32[192,2,128]{2,1,0:T(2,128)} %vis_ref.1, f32[192,2,128]{2,1,0:T(2,128)} %off_ref.1, f32[2,8,128]{2,1,0:T(8,128)} %pad.4.tile_ref), custom_call_target="tpu_custom_call" | custom-call | tf_op jit(solution)/shard_map/gather/pallas_call | solution.py:316
  57.2 59.6 %finish.1 = f32[2,4096,256]{2,1,0:T(8,128)} custom-call(f32[1536,32,128]{2,1,0:T(8,128)} %get-tuple-element.7.p_ref, f32[32,8,128]{2,1,0:T(8,128)} %get-tuple-element.8.ids_ref, f32[128,128]{1,0:T(8,128)} %constant.16.clone.phr_ref, f32[128,128]{1,0:T(8,128)} %constant.17.clone.phi_ref, bf16[32,128,128]{2,1,0:T(8,128)(2,1)} %constant.18.clone.waves_hbm, ...), custom_call_target="tpu_custom_call" | custom-call | tf_op jit(solution)/shard_map/finish/pallas_call | solution.py:553

commit v2 on v1

--- a/solution.py
+++ b/solution.py
@@ -18,13 +18,13 @@
 BF16 = jnp.bfloat16
 
 
-def _poly_coefs():
-    top = ((SUB - 4) / 2 / (2 * SUB)) ** 2
+def _poly_coefs(most, degree):
+    top = most**2
     nodes = top / 2 * (1 + np.cos(np.pi * (np.arange(64) + 0.5) / 64))
     r = np.sqrt(nodes)
     cheb = np.polynomial.chebyshev.Chebyshev
-    c = cheb.fit(nodes, np.cos(2 * np.pi * r), 4, domain=[0, top])
-    s = cheb.fit(nodes, np.sin(2 * np.pi * r) / r, 4, domain=[0, top])
+    c = cheb.fit(nodes, np.cos(2 * np.pi * r), degree, domain=[0, top])
+    s = cheb.fit(nodes, np.sin(2 * np.pi * r) / r, degree, domain=[0, top])
     poly = np.polynomial.Polynomial
     return (
         [float(v) for v in c.convert(kind=poly).coef],
@@ -32,16 +32,16 @@
     )
 
 
-COS_C, SIN_C = _poly_coefs()
-
-
-def cis(r):
+ANY_TURN = _poly_coefs(0.5, 5)
+SMALL_TURN = _poly_coefs((SUB / 2 - 2) / (2 * SUB), 4)
+
+
+def cis(r, coefs):
     z = r * r
-    c = COS_C[4]
-    s = SIN_C[4]
-    for k in range(3, -1, -1):
-        c = c * z + COS_C[k]
-        s = s * z + SIN_C[k]
+    c, s = coefs[0][-1], coefs[1][-1]
+    for k in range(len(coefs[0]) - 2, -1, -1):
+        c = c * z + coefs[0][k]
+        s = s * z + coefs[1][k]
     return c, s * r
 
 
@@ -82,50 +82,56 @@
 
 def pixel_rows(raw_ref, size, out_ref, row_ref, wave_ref):
     lane = lax.broadcasted_iota(jnp.int32, (SUB, VIS), 1)
+    step = (lax.broadcasted_iota(jnp.int32, (8, VIS), 0).astype(F32) + 0.5) / SUB
     cat = jnp.concatenate
 
     def prepare(t):
         ar, ai, u, v = (raw_ref[q * size + t * 8 : q * size + t * 8 + 8] for q in range(4))
-        firsts, steps = [], []
-        for axis, offset in enumerate((u, v)):
-            base = cis((offset - HALF) * (1.0 / (2 * SUB)))
-            twice = cmul(base, base)
-            wave = base
-            for m in range(8):
-                if m:
-                    wave = cmul(wave, twice)
-                for part in range(2):
-                    row = t * 8 * SUB + (axis * 2 + part) * 8 + m
-                    wave_ref[pl.ds(row, 8, stride=SUB), :] = wave[part]
-            firsts.append(base)
-            steps.append(cmul(wave, base))
-        pr, pi = cmul(*firsts)
-        rows = [*steps[0], *steps[1], ar * pr + ai * pi, ai * pr - ar * pi]
+        first_u, first_v = (cis((x - HALF) * (1.0 / (2 * SUB)), SMALL_TURN) for x in (u, v))
+        twice = cmul(first_u, first_u)
+        wave = first_u
+        for m in range(8):
+            if m:
+                wave = cmul(wave, twice)
+            for part in range(2):
+                row = t * 8 * 16 + part * 8 + m
+                wave_ref[pl.ds(row, 8, stride=16), :] = wave[part]
+        step_u = cmul(wave, first_u)
+        step_v = first_v
+        for _ in range(4):
+            step_v = cmul(step_v, step_v)
+        pr, pi = cmul(first_u, first_v)
+        rows = [*step_u, *step_v, ar * pr + ai * pi, ai * pr - ar * pi, v - HALF]
         for q, row in enumerate(rows):
             row_ref[t, q] = row
 
     def parts(n):
         t, d = n // 8, n % 8
         bc = lambda q: jnp.broadcast_to(row_ref[t, q, d : d + 1, :], (8, VIS))
-        ur, ui, vr, vi, ar, ai = (bc(q) for q in range(6))
-        cu, su, cv, sv = (wave_ref[n * SUB + q * 8 : n * SUB + q * 8 + 8] for q in range(4))
+        ur, ui, vr, vi, ar, ai, v = (bc(q) for q in range(7))
+        cu, su = (wave_ref[n * 16 + q * 8 : n * 16 + q * 8 + 8] for q in range(2))
+        turns = v * step
+        cv, sv = cis(turns - jnp.round(turns), ANY_TURN)
         ahead = lambda c, s, r, i: [c, c * r - s * i, s, c * i + s * r]
         us = ahead(cu, su, ur, ui)
         vs = ahead(cv, sv, vr, vi)
-        bs = [ar * x for x in vs] + [ai * x for x in vs]
-        uh, ul = split(cat(us, 0))
-        bh, bl = split(cat(bs, 0))
-        return cat([uh, ul, uh], 1), cat([bh, bh, bl], 1)
+        wh, wl = split(cat([ar * x for x in us] + [ai * x for x in us], 0))
+        vh, vl = split(cat(vs, 0))
+        return cat([wh, wl], 1), cat([vh, vh], 1), cat([vl, vl], 1)
 
     def pair(n):
         one, two = parts(n), parts(n + 1)
         prod = lax.dot_general(
             cat([one[0], two[0]], 0),
-            cat([one[1], two[1]], 0),
+            cat([one[1], two[1], one[2], two[2]], 0),
             (((1,), (1,)), ((), ())),
             preferred_element_type=F32,
         )
-        out_ref[n // 2] = jnp.where(lane < 64, prod[:SUB], prod[SUB:])
+        ar, ai, br, bi = (prod[q * SUB : q * SUB + SUB] for q in range(4))
+        fold = lambda p, q, r, s: jnp.where(
+            lane < 64, jnp.where(lane < 32, p, q), jnp.where(lane < 96, r, s)
+        )
+        out_ref[n // 2] = fold(ar, bi, ai, br) + pltpu.roll(fold(ai, br, ar, bi), 64, 1)
 
     prepare(0)
     for t in range(size // 8):
@@ -323,8 +329,8 @@
         out_specs=[anywhere, anywhere],
         scratch_shapes=[
             pltpu.VMEM((wide // 2, pieces, 4 * size + 8, 128), F32),
-            pltpu.VMEM((size // 8, 6, 8, VIS), F32),
-            pltpu.VMEM((size * SUB, VIS), F32),
+            pltpu.VMEM((size // 8, 7, 8, VIS), F32),
+            pltpu.VMEM((size * 16, VIS), F32),
             pltpu.VMEM((2, size // 2, SUB, 128), F32),
             dma((depth, pieces, 3)),
             dma((wide // 2, pieces)),
@@ -403,20 +409,20 @@
 
         lax.fori_loop(0, TILES, zero, 0)
         load.wait()
-        tab_ref[192:256] = jnp.zeros((64, 2 * nc), BF16)
+        tab_ref[...] = jnp.zeros(tab_ref.shape, BF16)
         for n in range(halves):
             left = slice(n * 128, n * 128 + 128)
             right = slice(nc + n * 128, nc + n * 128 + 128)
-            for part in range(3):
-                dr = wave_ref[n, part // 2 * 64 : part // 2 * 64 + 32]
-                di = wave_ref[n, part // 2 * 64 + 32 : part // 2 * 64 + 64]
-                tab_ref[part * 64 : part * 64 + 32, left] = dr
-                tab_ref[part * 64 + 32 : part * 64 + 64, left] = -di
-                tab_ref[part * 64 : part * 64 + 32, right] = di
-                tab_ref[part * 64 + 32 : part * 64 + 64, right] = dr
+            for row, low in ((0, 0), (32, 0), (128, 64)):
+                dr = wave_ref[n, low : low + 32]
+                di = wave_ref[n, low + 32 : low + 64]
+                tab_ref[row : row + 32, left] = dr
+                tab_ref[row : row + 32, right] = di
+                tab_ref[row + 64 : row + 96, left] = -di
+                tab_ref[row + 64 : row + 96, right] = dr
         scalars.wait()
 
-    lane = lax.broadcasted_iota(jnp.int32, (rows, 128), 1)
+    early = lax.broadcasted_iota(jnp.int32, (rows, 128), 1) % 64 < 32
 
     def multiply(t, slot):
         p = p_ref[pl.ds(t * chunk // 2, chunk // 2)].reshape(rows, 128)
@@ -424,10 +430,9 @@
         hif = hi.astype(F32)
         lof = p - hif
         lo = lof.astype(BF16)
-        hir = pltpu.roll(hi, 64, 1)
-        lor = pltpu.roll(lo, 64, 1)
-        one = jnp.where(lane < 64, hi, lor)
-        two = jnp.where(lane < 64, hir, lo)
+        hir = pltpu.roll(hi, 32, 1)
+        one = jnp.where(early, hi, pltpu.roll(lo, 32, 1))
+        two = jnp.where(early, hir, pltpu.roll(lo, 64, 1))
         lhs = jnp.concatenate(
             [
                 jnp.concatenate([one, hi], 1),

time: 117 us -> 115 us (0.983)
  Pallas kernels: 115 us -> 113 us
    pallas_call x1, Pallas kernels: 55.8 us -> 53.4 us  [gather(): pl.pallas_call(functools.partial(gather_kernel, wide, subs, size, min(4,...]
where the time goes in v2:
time: 115 us; the launch traced here: 114 us
  Pallas kernels  113 us (98%)
    pallas_call x1, Pallas kernels, finish(): pl.pallas_call(functools.partial(finish_kernel, block, nc, TILES.bit_leng...  59.6 us
    pallas_call x1, Pallas kernels, gather(): pl.pallas_call(functools.partial(gather_kernel, wide, subs, size, min(4,...  53.4 us

profile of v2, /device:TPU:0, one launch (start us, length us, event | category | flops | bytes accessed | tf_op | source)
XLA Modules:
  0.0 114.4 jit_solution(665454115251663159)
XLA Ops:
  0.0 0.7 add_convert_fusion
  0.7 0.1 reshape.3
  0.8 0.6 pad.4.tile_ref
  1.4 53.4 %gather.1 = (f32[1536,32,128]{2,1,0:T(8,128)}, f32[32,8,128]{2,1,0:T(8,128)}) custom-call(s32[192]{0:T(256)} %count_ref.1, f32[192,2,128]{2,1,0:T(2,128)} %vis_ref.1, f32[192,2,128]{2,1,0:T(2,128)} %off_ref.1, f32[2,8,128]{2,1,0:T(8,128)} %pad.4.tile_ref), custom_call_target="tpu_custom_call" | custom-call | tf_op jit(solution)/shard_map/gather/pallas_call | solution.py:322
  54.8 59.6 %finish.1 = f32[2,4096,256]{2,1,0:T(8,128)} custom-call(f32[1536,32,128]{2,1,0:T(8,128)} %get-tuple-element.7.p_ref, f32[32,8,128]{2,1,0:T(8,128)} %get-tuple-element.8.ids_ref, f32[128,128]{1,0:T(8,128)} %constant.16.clone.phr_ref, f32[128,128]{1,0:T(8,128)} %constant.17.clone.phi_ref, bf16[32,128,128]{2,1,0:T(8,128)(2,1)} %constant.18.clone.waves_hbm, ...), custom_call_target="tpu_custom_call" | custom-call | tf_op jit(solution)/shard_map/finish/pallas_call | solution.py:558

commit v3 on v2

--- a/solution.py
+++ b/solution.py
@@ -142,13 +142,14 @@
 
 
 def gather_kernel(
-    wide, subs, size, lag, count_ref, vis_ref, off_ref, tile_ref, pix_hbm, ids_hbm,
+    wide, subs, size, count_ref, vis_ref, off_ref, tile_ref, pix_hbm, ids_hbm,
     raw_ref, row_ref, wave_ref, out_ref,
     send_sem, recv_sem, loc_sem, pix_send, pix_recv, id_loc, id_send, id_recv,
 ):
     depth = wide // 4
     pieces = subs // size
     trips = 2 * depth * pieces
+    relays = (depth - 1) * pieces
     me = lax.axis_index("wide")
     core, y, z = me % 2, (me // 2) % 2, me // 4
     place = lambda zz, yy, cc: (zz * 2 + yy) * 2 + cc
@@ -261,12 +262,17 @@
         return mine, theirs
 
     def body(number, carry):
-        s, piece = number // pieces, number % pieces
-        zz = order(s // 2)
-        yy = y + (s % 2) * (1 - 2 * y)
+        later = number - pieces
+        middle, end = later // 2, later - 2 * relays
+        in_middle, in_end = later >= 0, end >= 0
+        k = jnp.where(in_end, depth - 1, jnp.where(in_middle, middle // pieces + later % 2, 0))
+        piece = jnp.where(in_end, end, jnp.where(in_middle, middle % pieces, number))
+        other = jnp.where(in_end, 1, jnp.where(in_middle, 1 - later % 2, 0))
+        zz = order(k)
+        yy = y + other * (1 - 2 * y)
         chip = zz * 2 + yy
 
-        @pl.when(s % 2 == 1)
+        @pl.when(other == 1)
         def _():
             hop(zz, yy, piece, across, 2).wait_recv()
 
@@ -283,9 +289,9 @@
         for copy in copies(number, chip, piece):
             copy.start()
 
-        @pl.when((number >= lag) & (number < lag + (depth - 1) * pieces))
+        @pl.when((number % 2 == 1) & (number // 2 < relays))
         def _():
-            pass_on(number - lag)
+            pass_on(number // 2)
 
         return carry
 
@@ -320,7 +326,7 @@
     anywhere = pl.BlockSpec(memory_space=pl.ANY)
     whole = pl.BlockSpec(memory_space=pltpu.VMEM)
     return pl.pallas_call(
-        functools.partial(gather_kernel, wide, subs, size, min(4, 2 * pieces - 1)),
+        functools.partial(gather_kernel, wide, subs, size),
         out_shape=[
             jax.ShapeDtypeStruct((wide * subs // 2, SUB, 128), F32),
             jax.ShapeDtypeStruct((wide * pieces, 8, 128), F32),
@@ -377,7 +383,7 @@
 
 
 def finish_kernel(
-    block, nc, shift, p_ref, ids_ref, phr_ref, phi_ref, waves_hbm, mix_hbm, out_hbm,
+    block, size, nc, shift, p_ref, ids_ref, phr_ref, phi_ref, waves_hbm, mix_hbm, out_hbm,
     x_ref, b_ref, y_ref, tab_ref, wave_ref, mix_ref, idv_ref, ids_smem, sem, id_sem, mix_sem, out_sem,
 ):
     g = pl.program_id(0)
@@ -444,7 +450,8 @@
 
     def add(t, slot):
         for d in range(chunk):
-            tile = ids_smem[g, t * chunk + d]
+            at = t * chunk + d
+            tile = ids_smem[g * (block // size) + at // size, at % size]
             r = lax.shift_right_logical(tile, shift)
             c = lax.bitwise_and(tile, TILES - 1)
             pr = jnp.broadcast_to(phr_ref[pl.ds(c, 1), :], (8, 128))
@@ -548,15 +555,16 @@
             store.wait()
 
 
-def finish(pix, ids, phr, phi, waves, mix, nc, block):
+def finish(pix, ids, phr, phi, waves, mix, nc, size):
     count = pix.shape[0] * 2
+    block = math.gcd(count, 2 * size)
     tiles = 2 * nc // 128
     const = lambda shape: pl.BlockSpec(shape, lambda g: (0,) * len(shape))
     anywhere = pl.BlockSpec(memory_space=pl.ANY)
     x_shape = (tiles, GRID, 128)
     dma = pltpu.SemaphoreType.DMA
     return pl.pallas_call(
-        functools.partial(finish_kernel, block, nc, TILES.bit_length() - 1),
+        functools.partial(finish_kernel, block, size, nc, TILES.bit_length() - 1),
         out_shape=jax.ShapeDtypeStruct((2, GRID, nc), F32),
         grid=(count // block,),
         in_specs=[
@@ -575,8 +583,8 @@
             pltpu.VMEM((256, 2 * nc), BF16),
             pltpu.VMEM((nc // 128, 128, 128), BF16),
             pltpu.VMEM(mix.shape, BF16),
-            pltpu.VMEM((count // block, 128), jnp.int32),
-            pltpu.SMEM((count // block, 128), jnp.int32),
+            pltpu.VMEM((count // size, 128), jnp.int32),
+            pltpu.SMEM((count // size, 128), jnp.int32),
             dma,
             dma,
             dma,

time: 115 us -> 106 us (0.922)
  the two profiles are of different devices: /device:TPU:0 before, /device:TPU:17 now
where the time goes in v3:
time: 106 us
  Pallas kernels  104 us (98%)
    pallas_call x1, Pallas kernels, finish(): pl.pallas_call(functools.partial(finish_kernel, block, size, nc, TILES.bi...  56.6 us
    pallas_call x1, Pallas kernels, gather(): pl.pallas_call(functools.partial(gather_kernel, wide, subs, size), out_sh...  47.9 us

profile of v3, /device:TPU:17, one launch (start us, length us, event | category | flops | bytes accessed | tf_op | source)
XLA Modules:
  0.0 105.9 jit_solution(18114501009780913308)
XLA Ops:
  0.0 0.7 add_convert_fusion
  0.7 0.1 reshape.3
  0.8 0.6 pad.4.tile_ref
  1.4 47.9 %gather.1 = (f32[1536,32,128]{2,1,0:T(8,128)}, f32[32,8,128]{2,1,0:T(8,128)}) custom-call(s32[192]{0:T(256)} %count_ref.1, f32[192,2,128]{2,1,0:T(2,128)} %vis_ref.1, f32[192,2,128]{2,1,0:T(2,128)} %off_ref.1, f32[2,8,128]{2,1,0:T(8,128)} %pad.4.tile_ref), custom_call_target="tpu_custom_call" | custom-call | tf_op jit(solution)/shard_map/gather/pallas_call | solution.py:328
  49.3 56.6 %finish.1 = f32[2,4096,256]{2,1,0:T(8,128)} custom-call(f32[1536,32,128]{2,1,0:T(8,128)} %get-tuple-element.7.p_ref, f32[32,8,128]{2,1,0:T(8,128)} %get-tuple-element.8.ids_ref, f32[128,128]{1,0:T(8,128)} %constant.16.clone.phr_ref, f32[128,128]{1,0:T(8,128)} %constant.17.clone.phi_ref, bf16[32,128,128]{2,1,0:T(8,128)(2,1)} %constant.18.clone.waves_hbm, ...), custom_call_target="tpu_custom_call" | custom-call | tf_op jit(solution)/shard_map/finish/pallas_call | solution.py:566

commit v4 on v3

--- a/solution.py
+++ b/solution.py
@@ -142,7 +142,8 @@
 
 
 def gather_kernel(
-    wide, subs, size, count_ref, vis_ref, off_ref, tile_ref, pix_hbm, ids_hbm,
+    wide, subs, size, band, count_ref, owner_ref, row_in_ref, col_ref, vis_ref, off_ref,
+    pix_hbm, ids_hbm,
     raw_ref, row_ref, wave_ref, out_ref,
     send_sem, recv_sem, loc_sem, pix_send, pix_recv, id_loc, id_send, id_recv,
 ):
@@ -173,23 +174,23 @@
     def _():
         pl.semaphore_signal(barrier, inc=1, device_id=below, device_id_type=mesh_id)
 
-    slots = lax.broadcasted_iota(jnp.int32, (2, VIS), 1)
-
-    def stage(t, carry):
-        piece = t * 8 // size
-        base = t * 8 - piece * size
-        for d in range(8):
-            n = t * 8 + d
-            live = jnp.where(slots < count_ref[n], 1.0 / math.sqrt(VIS), 0.0)
-            for half, pair in enumerate((vis_ref[n] * live, off_ref[n])):
-                for q in range(2):
-                    row = (half * 2 + q) * size + base + d
-                    raw_ref[here, piece, pl.ds(row, 1), :] = pair[q : q + 1]
-        return carry
-
-    lax.fori_loop(0, subs // 8, stage, 0)
+    slots = lax.broadcasted_iota(jnp.int32, (8, VIS), 1)
     for piece in range(pieces):
-        raw_ref[here, piece, 4 * size :, :] = tile_ref[piece]
+
+        def stage(t, ids):
+            for d in range(8):
+                j = t * 8 + d
+                n = piece * size + j
+                live = jnp.where(slots[:2] < count_ref[n], 1.0 / math.sqrt(VIS), 0.0)
+                for half, pair in enumerate((vis_ref[n] * live, off_ref[n])):
+                    for q in range(2):
+                        raw_ref[here, piece, pl.ds((half * 2 + q) * size + j, 1), :] = pair[q : q + 1]
+                tile = (owner_ref[n] * band + row_in_ref[n]) * TILES + col_ref[n]
+                ids = jnp.where(slots == j, tile, ids)
+            return ids
+
+        ids = lax.fori_loop(0, size // 8, stage, jnp.zeros((8, VIS), jnp.int32))
+        raw_ref[here, piece, 4 * size :, :] = ids.astype(F32)
     neighbours = jnp.minimum(z, 1) + jnp.minimum(depth - 1 - z, 1)
     pl.semaphore_wait(barrier, 2 + neighbours)
 
@@ -227,8 +228,9 @@
                 hop(zz, y, piece, across, 2).wait_recv()
                 spread_out(zz, piece, lambda copy: copy.start())
 
+    near = jnp.minimum(z, depth - 1 - z)
+
     def order(k):
-        near = jnp.minimum(z, depth - 1 - z)
         swing = z + ((k + 1) // 2) * (1 - 2 * (k % 2))
         edge = jnp.where(z * 2 < depth - 1, k, depth - 1 - k)
         return jnp.where(k <= 2 * near, swing, edge)
@@ -263,11 +265,18 @@
 
     def body(number, carry):
         later = number - pieces
-        middle, end = later // 2, later - 2 * relays
-        in_middle, in_end = later >= 0, end >= 0
-        k = jnp.where(in_end, depth - 1, jnp.where(in_middle, middle // pieces + later % 2, 0))
-        piece = jnp.where(in_end, end, jnp.where(in_middle, middle % pieces, number))
-        other = jnp.where(in_end, 1, jnp.where(in_middle, 1 - later % 2, 0))
+        end = later - 2 * relays
+        other = jnp.where(later >= 0, jnp.where(end >= 0, 1, 1 - later % 2), 0)
+        at_turn = jnp.where(later >= 0, jnp.where(end >= 0, relays + end, later // 2), number)
+        relayed = jnp.where(later >= 0, 1 - other, 0)
+        relay = at_turn - pieces * (1 - relayed)
+        first = relay < 0
+        paired = relay < 2 * near * pieces
+        group = 2 * pieces
+        k = jnp.where(paired, 1 + relay // group * 2 + relay % 2, 1 + relay // pieces)
+        k = jnp.where(first, 0, k)
+        piece = jnp.where(paired, relay % group // 2, relay % pieces)
+        piece = jnp.where(first, at_turn, piece)
         zz = order(k)
         yy = y + other * (1 - 2 * y)
         chip = zz * 2 + yy
@@ -317,7 +326,7 @@
     lax.fori_loop(0, trips, arrive, 0)
 
 
-def gather(counts, visibilities, offsets, tile, wide, size):
+def gather(scalars, visibilities, offsets, wide, size, band):
     subs = visibilities.shape[0]
     depth = wide // 4
     pieces = subs // size
@@ -326,12 +335,12 @@
     anywhere = pl.BlockSpec(memory_space=pl.ANY)
     whole = pl.BlockSpec(memory_space=pltpu.VMEM)
     return pl.pallas_call(
-        functools.partial(gather_kernel, wide, subs, size),
+        functools.partial(gather_kernel, wide, subs, size, band),
         out_shape=[
             jax.ShapeDtypeStruct((wide * subs // 2, SUB, 128), F32),
             jax.ShapeDtypeStruct((wide * pieces, 8, 128), F32),
         ],
-        in_specs=[pl.BlockSpec(memory_space=pltpu.SMEM), whole, whole, whole],
+        in_specs=[pl.BlockSpec(memory_space=pltpu.SMEM)] * 4 + [whole, whole],
         out_specs=[anywhere, anywhere],
         scratch_shapes=[
             pltpu.VMEM((wide // 2, pieces, 4 * size + 8, 128), F32),
@@ -349,7 +358,7 @@
         ],
         compiler_params=pltpu.CompilerParams(collective_id=0, has_side_effects=True),
         name="gather",
-    )(counts, visibilities, offsets, tile)
+    )(*scalars, visibilities, offsets)
 
 
 def fft(xs):
@@ -617,9 +626,8 @@
     g, w = np_tables()
     subs = visibilities.shape[0]
     size = math.gcd(subs, 96)
-    tile = ((owner * band + tile_row) * TILES + tile_col).astype(F32)
-    tile = jnp.pad(tile.reshape(subs // size, 1, size), ((0, 0), (0, 7), (0, 128 - size)))
-    pix, ids = gather(vis_count, visibilities, offsets, tile, wide, size)
+    scalars = (vis_count, owner, tile_row, tile_col)
+    pix, ids = gather(scalars, visibilities, offsets, wide, size, band)
     m4 = real_form(shifted(g) / 256.0).transpose(4, 0, 2, 1, 3).reshape(TILES, 64, 64)
     both = jnp.asarray(np.concatenate(np_split(m4), 2))
     phr, phi = jnp.asarray(w.real, F32), jnp.asarray(w.imag, F32)

time: 106 us -> 102 us (0.962)
  the two profiles are of different devices: /device:TPU:17 before, /device:TPU:0 now
where the time goes in v4:
time: 102 us
  Pallas kernels  102 us (100%)
    pallas_call x1, Pallas kernels, finish(): pl.pallas_call(functools.partial(finish_kernel, block, size, nc, TILES.bi...  56.6 us
    pallas_call x1, Pallas kernels, gather(): pl.pallas_call(functools.partial(gather_kernel, wide, subs, size, band),...  45.7 us

profile of v4, /device:TPU:0, one launch (start us, length us, event | category | flops | bytes accessed | tf_op | source)
XLA Modules:
  0.0 102.3 jit_solution(12439510656163926234)
XLA Ops:
  0.0 45.7 %gather.1 = (f32[1536,32,128]{2,1,0:T(8,128)}, f32[32,8,128]{2,1,0:T(8,128)}) custom-call(s32[192]{0:T(256)} %count_ref.1, s32[192]{0:T(256)} %owner_ref.1, s32[192]{0:T(256)} %row_in_ref.1, s32[192]{0:T(256)} %col_ref.1, f32[192,2,128]{2,1,0:T(2,128)} %vis_ref.1, f32[192,2,128]{2,1,0:T(2,128)} %off_ref.1), custom_call_target="tpu_custom_call" | custom-call | tf_op jit(solution)/shard_map/gather/pallas_call | solution.py:337
  45.7 56.6 %finish.1 = f32[2,4096,256]{2,1,0:T(8,128)} custom-call(f32[1536,32,128]{2,1,0:T(8,128)} %get-tuple-element.7.p_ref, f32[32,8,128]{2,1,0:T(8,128)} %get-tuple-element.8.ids_ref, f32[128,128]{1,0:T(8,128)} %constant.9.clone.phr_ref, f32[128,128]{1,0:T(8,128)} %constant.10.clone.phi_ref, bf16[32,128,128]{2,1,0:T(8,128)(2,1)} %constant.11.clone.waves_hbm, ...), custom_call_target="tpu_custom_call" | custom-call | tf_op jit(solution)/shard_map/finish/pallas_call | solution.py:575

commit v5 on v4

--- a/solution.py
+++ b/solution.py
@@ -175,8 +175,7 @@
         pl.semaphore_signal(barrier, inc=1, device_id=below, device_id_type=mesh_id)
 
     slots = lax.broadcasted_iota(jnp.int32, (8, VIS), 1)
-    for piece in range(pieces):
-
+    def stage_piece(piece):
         def stage(t, ids):
             for d in range(8):
                 j = t * 8 + d
@@ -191,6 +190,8 @@
 
         ids = lax.fori_loop(0, size // 8, stage, jnp.zeros((8, VIS), jnp.int32))
         raw_ref[here, piece, 4 * size :, :] = ids.astype(F32)
+
+    stage_piece(0)
     neighbours = jnp.minimum(z, 1) + jnp.minimum(depth - 1 - z, 1)
     pl.semaphore_wait(barrier, 2 + neighbours)
 
@@ -216,8 +217,9 @@
         def _():
             act(hop(zz, y, piece, below, 1))
 
-    for piece in range(pieces):
-        spread_out(z, piece, lambda copy: copy.start())
+    spread_out(z, 0, lambda copy: copy.start())
+    for piece in range(1, pieces):
+        stage_piece(piece)
 
     def pass_on(number):
         far, piece = number // pieces + 1, number % pieces
@@ -297,6 +299,10 @@
         pixel_rows(raw_ref.at[chip, piece], size, out_ref.at[number % 2], row_ref, wave_ref)
         for copy in copies(number, chip, piece):
             copy.start()
+
+        @pl.when(number + 1 < pieces)
+        def _():
+            spread_out(z, number + 1, lambda copy: copy.start())
 
         @pl.when((number % 2 == 1) & (number // 2 < relays))
         def _():
@@ -521,14 +527,19 @@
                     b_ref[halves + n, pick, :] = i
             return carry
 
-        def mix(n, t, carry):
+        def mix(t, carry):
             parts = []
             for d in range(8):
                 m = t * 8 + d
                 near = pl.ds(pl.multiple_of(m * SUB, SUB), SUB)
-                zh, zl = split(
-                    jnp.concatenate([b_ref[o * halves + n, near, :] for o in range(2)], 0)
+                zm = jnp.concatenate(
+                    [
+                        jnp.concatenate([b_ref[o * halves + n, near, :] for n in range(halves)], 1)
+                        for o in range(2)
+                    ],
+                    0,
                 )
+                zh, zl = split(zm)
                 both = mix_ref[m]
                 res = jnp.dot(
                     jnp.concatenate([both, both[:, :64]], 1),
@@ -536,32 +547,37 @@
                     preferred_element_type=F32,
                 )
                 parts.append(res[None])
-            for q in range(8):
-                block8 = jnp.concatenate([p[:, q * 8 : q * 8 + 8] for p in parts], 0)
-                turned = jnp.transpose(block8, (1, 0, 2))
-                for e in range(8):
-                    p, b = divmod(q * 8 + e, SUB)
-                    far = pl.ds(pl.multiple_of(b * TILES + t * 8, 8), 8)
-                    x_ref[p * halves + n, far, :] = turned[e]
+            for n in range(halves):
+                for q in range(8):
+                    block8 = jnp.concatenate(
+                        [p[:, q * 8 : q * 8 + 8, n * 128 : n * 128 + 128] for p in parts], 0
+                    )
+                    turned = jnp.transpose(block8, (1, 0, 2))
+                    for e in range(8):
+                        p, b = divmod(q * 8 + e, SUB)
+                        far = pl.ds(pl.multiple_of(b * TILES + t * 8, 8), 8)
+                        x_ref[p * halves + n, far, :] = turned[e]
+            rows8 = pl.ds(pl.multiple_of(t * 8, 8), 8)
+            for p in range(2):
+                for n in range(halves):
+                    pltpu.make_async_copy(
+                        x_ref.reshape(2 * halves, SUB, TILES, 128).at[p * halves + n, :, rows8],
+                        out_hbm.reshape(2, SUB, TILES, nc).at[p, :, rows8, pl.ds(n * 128, 128)],
+                        out_sem.at[p * halves + n],
+                    ).start()
             return carry
 
-        stores = []
-        for n in range(halves):
-            lax.fori_loop(4 * n, 4 * n + 4, eights, 0)
-            lax.fori_loop(4 * n, 4 * n + 4, sixteens, 0)
-            if n == 0:
-                pltpu.make_async_copy(mix_hbm, mix_ref, mix_sem).wait()
-            lax.fori_loop(0, TILES // 8, functools.partial(mix, n), 0)
-            for p in range(2):
-                store = pltpu.make_async_copy(
+        lax.fori_loop(0, 4 * halves, eights, 0)
+        lax.fori_loop(0, 4 * halves, sixteens, 0)
+        pltpu.make_async_copy(mix_hbm, mix_ref, mix_sem).wait()
+        lax.fori_loop(0, TILES // 8, mix, 0)
+        for p in range(2):
+            for n in range(halves):
+                pltpu.make_async_copy(
                     x_ref.at[p * halves + n],
                     out_hbm.at[p, :, pl.ds(n * 128, 128)],
                     out_sem.at[p * halves + n],
-                )
-                store.start()
-                stores.append(store)
-        for store in stores:
-            store.wait()
+                ).wait()
 
 
 def finish(pix, ids, phr, phi, waves, mix, nc, size):

time: 102 us -> 97.3 us (0.954)
  Pallas kernels: 102 us -> 97.2 us
    pallas_call x1, Pallas kernels: 56.6 us -> 51.5 us  [finish(): pl.pallas_call(functools.partial(finish_kernel, block, size, nc, TILES.bi...]
where the time goes in v5:
time: 97.3 us; the launch traced here: 97.2 us
  Pallas kernels  97.2 us (100%)
    pallas_call x1, Pallas kernels, finish(): pl.pallas_call(functools.partial(finish_kernel, block, size, nc, TILES.bi...  51.5 us
    pallas_call x1, Pallas kernels, gather(): pl.pallas_call(functools.partial(gather_kernel, wide, subs, size, band),...  45.7 us

profile of v5, /device:TPU:0, one launch (start us, length us, event | category | flops | bytes accessed | tf_op | source)
XLA Modules:
  0.0 97.2 jit_solution(11037155182902887495)
XLA Ops:
  0.0 45.7 %gather.1 = (f32[1536,32,128]{2,1,0:T(8,128)}, f32[32,8,128]{2,1,0:T(8,128)}) custom-call(s32[192]{0:T(256)} %count_ref.1, s32[192]{0:T(256)} %owner_ref.1, s32[192]{0:T(256)} %row_in_ref.1, s32[192]{0:T(256)} %col_ref.1, f32[192,2,128]{2,1,0:T(2,128)} %vis_ref.1, f32[192,2,128]{2,1,0:T(2,128)} %off_ref.1), custom_call_target="tpu_custom_call" | custom-call | tf_op jit(solution)/shard_map/gather/pallas_call | solution.py:343
  45.7 51.5 %finish.1 = f32[2,4096,256]{2,1,0:T(8,128)} custom-call(f32[1536,32,128]{2,1,0:T(8,128)} %get-tuple-element.7.p_ref, f32[32,8,128]{2,1,0:T(8,128)} %get-tuple-element.8.ids_ref, f32[128,128]{1,0:T(8,128)} %constant.9.clone.phr_ref, f32[128,128]{1,0:T(8,128)} %constant.10.clone.phi_ref, bf16[32,128,128]{2,1,0:T(8,128)(2,1)} %constant.11.clone.waves_hbm, ...), custom_call_target="tpu_custom_call" | custom-call | tf_op jit(solution)/shard_map/finish/pallas_call | solution.py:591

commit v6 on v5

--- a/solution.py
+++ b/solution.py
@@ -80,7 +80,7 @@
     return to_waves(g[index])
 
 
-def pixel_rows(raw_ref, size, out_ref, row_ref, wave_ref):
+def pixel_rows(raw_ref, size, out_ref, row_ref, wave_ref, send):
     lane = lax.broadcasted_iota(jnp.int32, (SUB, VIS), 1)
     step = (lax.broadcasted_iota(jnp.int32, (8, VIS), 0).astype(F32) + 0.5) / SUB
     cat = jnp.concatenate
@@ -139,6 +139,8 @@
             prepare(t + 1)
         for d in range(0, 8, 2):
             pair(t * 8 + d)
+        if (t + 1) * 16 % size == 0:
+            send((t + 1) * 16 // size - 1)
 
 
 def gather_kernel(
@@ -237,15 +239,17 @@
         edge = jnp.where(z * 2 < depth - 1, k, depth - 1 - k)
         return jnp.where(k <= 2 * near, swing, edge)
 
-    def copies(number, chip, piece):
-        rows = pl.ds(((chip * 2 + core) * subs + piece * size) // 2, size // 2)
-        slot = number % 2
-        mine = pltpu.make_async_copy(out_ref.at[slot], pix_hbm.at[rows], loc_sem.at[slot])
+    def copies(number, chip, piece, half):
+        part = size // 4
+        rows = pl.ds(((chip * 2 + core) * subs + piece * size) // 2 + half * part, part)
+        slot = number % 2 * 2 + half
+        block = out_ref.at[number % 2, pl.ds(half * part, part)]
+        mine = pltpu.make_async_copy(block, pix_hbm.at[rows], loc_sem.at[slot])
         theirs = pltpu.make_async_remote_copy(
-            src_ref=out_ref.at[slot],
+            src_ref=block,
             dst_ref=pix_hbm.at[rows],
             send_sem=pix_send.at[slot],
-            recv_sem=pix_recv.at[number],
+            recv_sem=pix_recv.at[number * 2 + half],
             device_id=partner,
             device_id_type=mesh_id,
         )
@@ -292,13 +296,16 @@
 
         @pl.when(number >= 2)
         def _():
-            mine, theirs = copies(number, chip, piece)
-            mine.wait()
-            theirs.wait_send()
-
-        pixel_rows(raw_ref.at[chip, piece], size, out_ref.at[number % 2], row_ref, wave_ref)
-        for copy in copies(number, chip, piece):
-            copy.start()
+            for half in range(2):
+                mine, theirs = copies(number, chip, piece, half)
+                mine.wait()
+                theirs.wait_send()
+
+        def send(half):
+            for copy in copies(number, chip, piece, half):
+                copy.start()
+
+        pixel_rows(raw_ref.at[chip, piece], size, out_ref.at[number % 2], row_ref, wave_ref, send)
 
         @pl.when(number + 1 < pieces)
         def _():
@@ -318,15 +325,17 @@
 
     lax.fori_loop(0, depth * pieces, drain, 0)
     for number in range(2):
-        mine, theirs = copies(number, here, 0)
-        mine.wait()
-        theirs.wait_send()
+        for half in range(2):
+            mine, theirs = copies(number, here, 0, half)
+            mine.wait()
+            theirs.wait_send()
 
     def arrive(number, carry):
         mine, theirs = id_copies(number, here, 0)
         mine.wait()
         theirs.wait()
-        copies(number, here, 0)[1].wait_recv()
+        for half in range(2):
+            copies(number, here, 0, half)[1].wait_recv()
         return carry
 
     lax.fori_loop(0, trips, arrive, 0)
@@ -355,9 +364,9 @@
             pltpu.VMEM((2, size // 2, SUB, 128), F32),
             dma((depth, pieces, 3)),
             dma((wide // 2, pieces)),
-            dma((2,)),
-            dma((2,)),
-            dma((trips,)),
+            dma((4,)),
+            dma((4,)),
+            dma((2 * trips,)),
             dma((trips,)),
             dma((trips,)),
             dma((trips,)),

time: 97.3 us -> 98.4 us (1.011)
    pallas_call x1, Pallas kernels: 45.7 us -> 46.8 us  [gather(): pl.pallas_call(functools.partial(gather_kernel, wide, subs, size, band),...]
where the time goes in v6:
time: 98.4 us; the launch traced here: 98.1 us
  Pallas kernels  98.1 us (100%)
    pallas_call x1, Pallas kernels, finish(): pl.pallas_call(functools.partial(finish_kernel, block, size, nc, TILES.bi...  51.3 us
    pallas_call x1, Pallas kernels, gather(): pl.pallas_call(functools.partial(gather_kernel, wide, subs, size, band),...  46.8 us

profile of v6, /device:TPU:0, one launch (start us, length us, event | category | flops | bytes accessed | tf_op | source)
XLA Modules:
  0.0 98.1 jit_solution(15056928221651494848)
XLA Ops:
  0.0 46.8 %gather.1 = (f32[1536,32,128]{2,1,0:T(8,128)}, f32[32,8,128]{2,1,0:T(8,128)}) custom-call(s32[192]{0:T(256)} %count_ref.1, s32[192]{0:T(256)} %owner_ref.1, s32[192]{0:T(256)} %row_in_ref.1, s32[192]{0:T(256)} %col_ref.1, f32[192,2,128]{2,1,0:T(2,128)} %vis_ref.1, f32[192,2,128]{2,1,0:T(2,128)} %off_ref.1), custom_call_target="tpu_custom_call" | custom-call | tf_op jit(solution)/shard_map/gather/pallas_call | solution.py:352
  46.9 51.3 %finish.1 = f32[2,4096,256]{2,1,0:T(8,128)} custom-call(f32[1536,32,128]{2,1,0:T(8,128)} %get-tuple-element.7.p_ref, f32[32,8,128]{2,1,0:T(8,128)} %get-tuple-element.8.ids_ref, f32[128,128]{1,0:T(8,128)} %constant.9.clone.phr_ref, f32[128,128]{1,0:T(8,128)} %constant.10.clone.phi_ref, bf16[32,128,128]{2,1,0:T(8,128)(2,1)} %constant.11.clone.waves_hbm, ...), custom_call_target="tpu_custom_call" | custom-call | tf_op jit(solution)/shard_map/finish/pallas_call | solution.py:600
